TPU v7x, 32 devices: a whole 2x2x4 slice. The times are simulated.
32 devices in a mesh: zone: 4 (over y, x), slab: 8 (over z, core).
Axes of the slice: x: 2, y: 2, z: 4, core: 2. Of those that a mesh axis runs over, the one named last changes fastest.
Arguments:
- tracers: float32 [4, 4, 2048, 2048], P('zone', None, 'slab'), may hold values from -6 to 6
- velocity: float32 [4, 2, 2048, 2048], P('zone', None, 'slab'), may hold values from -0.2 to 0.2
- diffusivity: float32 [4], replicated, may hold values from 0.02 to 0.12
- owner_dev: int32 [512, 2], P('slab'), may hold values from 0 to 23, all different within a row; in each aligned block of 64 rows (0 to 63, 64 to 127, ...) at most 7 rows name the same one
- owner_seg: int32 [512, 2], P('slab'), may hold values from 0 to 63
- intersection: float32 [512, 2], P('slab'), may hold values from 0.2 to 1
Outputs:
- updated: float32 [4, 4, 2048, 2048], P('zone', None, 'slab')
Inputs may be any that keep to these rules, and one draw needn't show every extreme that they name: owner_dev names workpiece slab zone * 8 + slab; the 2 entries of a row differ; the rows of one pin slab name one workpiece slab at most 7 times, and some name one exactly 7 times.
All inputs are finite; a program needn't handle non-finite values.
Results may differ from a plain program's by a relative error of at most 0.00007.
Values sent between devices are 32-bit elements; how exact they have to be, the bound alone decides.
No kernel may reach another device: no remote copies, remote signals or barrier semaphores. Data moves between devices by JAX's collectives and lax.ppermute only.
A program may use at most 128 MiB of HBM per device.

v0:
```python
import jax
import jax.numpy as jnp
from jax import lax
from jax.sharding import PartitionSpec as P

SEG = 32
COUPLE = 0.5


def extended(block, sides, width):
    for axis, dim in sides:
        count = lax.axis_size(axis)
        forward = [(i, i + 1) for i in range(count - 1)]
        backward = [(target, source) for source, target in forward]
        low = lax.ppermute(
            lax.slice_in_dim(block, block.shape[dim] - width, None, axis=dim), axis, forward
        )
        high = lax.ppermute(lax.slice_in_dim(block, 0, width, axis=dim), axis, backward)
        block = jnp.concatenate([low, block, high], axis=dim)
    return block


def from_root(block, axis, owner):
    block = jnp.where(lax.axis_index(axis) == owner, block, jnp.zeros_like(block))
    return lax.psum(block, axis)


def advance(center, upper_row, lower_row, velocity, diffusivity):
    left_cells = jnp.roll(center, 1, axis=3)
    right_cells = jnp.roll(center, -1, axis=3)
    along_rows = velocity[:, 0][:, None]
    along_cols = velocity[:, 1][:, None]
    transport = jnp.maximum(along_rows, 0.0) * (center - upper_row) + jnp.minimum(
        along_rows, 0.0
    ) * (lower_row - center)
    transport = (
        transport
        + jnp.maximum(along_cols, 0.0) * (center - left_cells)
        + jnp.minimum(along_cols, 0.0) * (right_cells - center)
    )
    laplace = upper_row + lower_row + left_cells + right_cells - 4.0 * center
    return center + diffusivity[None, :, None, None] * laplace - transport


def shards(tracers, velocity, diffusivity, owner_dev, owner_seg, intersection):
    zone_count = lax.axis_size("zone")
    slab_count = lax.axis_size("slab")
    zone_index = lax.axis_index("zone")
    padded = extended(tracers, (("slab", 2),), 1)
    stepped = advance(
        padded[:, :, 1:-1], padded[:, :, :-2], padded[:, :, 2:], velocity, diffusivity
    )
    tracer_count = tracers.shape[1]
    row_count = tracers.shape[2]
    col_count = tracers.shape[3]
    seg_count = col_count // SEG
    payload = tracer_count * SEG
    own_face = (
        tracers[0, :, row_count - 1, :]
        .reshape(tracer_count, seg_count, SEG)
        .transpose(1, 0, 2)
        .reshape(seg_count, payload)
    )
    pin_face = from_root(own_face, "zone", zone_count - 1)
    fanout = owner_dev.shape[1]
    item_count = owner_dev.shape[0] * fanout
    target_dev = owner_dev.reshape(item_count)
    target_seg = owner_seg.reshape(item_count)
    weight = intersection.reshape(item_count)
    in_zone = target_dev // slab_count == zone_index
    target_slab = target_dev % slab_count
    pin_values = jnp.repeat(pin_face, fanout, axis=0)
    highest = lax.Precision.HIGHEST
    zone_faces = lax.all_gather(own_face, "slab", axis=0, tiled=True)
    slot_ids = jnp.arange(slab_count * seg_count, dtype=jnp.int32)
    picker = (
        ((target_slab * seg_count + target_seg)[:, None] == slot_ids[None, :]) & in_zone[:, None]
    ).astype(jnp.float32)
    owner_values = jnp.dot(picker, zone_faces, precision=highest)
    item_flux = jnp.where(in_zone, weight, 0.0)[:, None] * (pin_values - owner_values)
    inflow = lax.psum_scatter(
        jnp.dot(picker.T, item_flux, precision=highest), "slab", scatter_dimension=0, tiled=True
    )
    pin_part = jnp.sum(item_flux.reshape(seg_count, fanout, payload), axis=1)
    pin_total = lax.psum(pin_part, "zone")
    is_pin = zone_index == zone_count - 1
    coupling = COUPLE * inflow - jnp.where(is_pin, COUPLE * pin_total, 0.0)
    coupling = (
        coupling.reshape(seg_count, tracer_count, SEG)
        .transpose(1, 0, 2)
        .reshape(tracer_count, col_count)
    )
    return stepped.at[0, :, row_count - 1, :].add(coupling)


def solution(mesh):
    placed = (
        P("zone", None, "slab", None),
        P("zone", None, "slab", None),
        P(),
        P("slab", None),
        P("slab", None),
        P("slab", None),
    )
    return jax.shard_map(
        shards, mesh=mesh, in_specs=placed, out_specs=P("zone", None, "slab", None), check_vma=False
    )
```

profile of v0, /device:TPU:8, one launch (start us, length us, event | category | flops | bytes accessed | tf_op | source)
XLA Modules:
  0.0 117.2 jit_solution(10784930607515676139)
XLA Ops:
  6.5 0.0 reduce-scatter.2.cloned.1.call-start
  6.5 1.2 slice_reduce_fusion
  7.7 0.1 reshape_squeeze.3
  7.8 0.1 copy.60
  7.9 0.1 copy.61
  7.9 14.4 %all_gather.3 = f32[512,128]{1,0:T(8,128)S(1)} all-gather(f32[64,128]{1,0:T(8,128)S(1)} %copy.61), channel_id=1, replica_groups=mesh['zone'=4,'slab'=8] {'slab'}, dimensions={0}, use_global_device_ids=true | all-gather | bytes 294912 | tf_op jit(solution)/shard_map/all_gather | solution.py:74
  22.4 16.3 %psum.14 = f32[64,128]{1,0:T(8,128)S(1)} all-reduce(f32[64,128]{1,0:T(8,128)S(1)} %broadcast_select_fusion.1), channel_id=1, replica_groups=mesh['zone'=4,'slab'=8] {'zone'}, use_global_device_ids=true, to_apply=%region_1.2 | all-reduce | flops 8192 | bytes 65536 | tf_op jit(solution)/shard_map/psum | solution.py:25
  38.7 0.8 copy.57
  39.5 0.1 reshape.148
  39.6 0.8 copy.59
  40.4 0.1 reshape.150
  40.5 0.8 copy.58
  41.3 0.1 reshape.149
  41.5 0.3 fusion.14
  41.8 1.2 fusion.16
  43.0 0.0 reduce-scatter.2.cloned.1.call-update
  43.0 1.9 %collective-permute-start = (f32[1,4,1,2048]{3,2,1,0:T(1,128)S(1)}, f32[1,4,1,2048]{3,2,1,0:T(1,128)S(1)}, u32[]{:S(2)}, u32[]{:S(2)}) collective-permute-start(f32[1,4,1,2048]{3,2,1,0:T(1,128)S(1)} %get-tuple-element.21), channel_id=1, source_target_pairs={{0,1},{1,2},{2,3},{3,4},{4,5},{5,6},{6,7},{8,9},{9,10},{10,11},{11... | collective-permute-start | bytes 98312 | tf_op jit(solution)/shard_map/ppermute | solution.py:15
  44.9 0.0 copy-start
  44.9 3.9 %collective-permute-start.1 = (f32[1,4,1,2048]{3,2,1,0:T(1,128)S(1)}, f32[1,4,1,2048]{3,2,1,0:T(1,128)S(1)}, u32[]{:S(2)}, u32[]{:S(2)}) collective-permute-start(f32[1,4,1,2048]{3,2,1,0:T(1,128)S(1)} %get-tuple-element.20), channel_id=1, source_target_pairs={{1,0},{2,1},{3,2},{4,3},{5,4},{6,5},{7,6},{9,8},{10,9},{11,10},{12... | collective-permute-start | bytes 98312 | tf_op jit(solution)/shard_map/ppermute | solution.py:18
  48.9 13.3 %fusion.28 = (f32[1,4,256,2047]{3,2,1,0:T(8,128)}, f32[1,4,256,2047]{3,2,1,0:T(8,128)}) fusion(f32[1,4,256,2048]{3,2,1,0:T(8,128)} %param.8), kind=kLoop, calls=%fused_computation.47 | loop fusion | bytes 33538048 | tf_op jit(solution)/shard_map/jit(_roll_static)/slice | solution.py:29
  62.1 0.0 copy-start.2
  62.1 0.0 copy-start.1
  62.1 1.4 %fusion.27 = (f32[1,4,256,1]{3,2,1,0:T(8,128)S(1)}, f32[1,4,256,1]{3,2,1,0:T(8,128)S(1)}) fusion(f32[1,4,256,2048]{3,2,1,0:T(8,128)} %param.8), kind=kLoop, calls=%fused_computation.46 | loop fusion | bytes 16384 | tf_op jit(solution)/shard_map/jit(_roll_static)/slice | solution.py:29
  63.6 0.0 copy-done
  63.6 2.9 %maximum_bitcast_fusion.1 = (f32[256,2048]{1,0:T(8,128)S(1)}, f32[256,2048]{1,0:T(8,128)}, f32[256,2048]{1,0:T(8,128)}, f32[256,2048]{1,0:T(8,128)}) fusion(f32[1,2,256,2048]{3,2,1,0:T(8,128)S(1)} %copy-done), kind=kLoop, calls=%fused_computation.21 | loop fusion | flops 2097152 | bytes 12582912 | tf_op jit(solution)/shard_map/mul | solution.py:33
  66.5 0.6 fusion.29
  67.1 0.0 copy-done.2
  67.1 2.0 %and_reduce_fusion = pred[]{:T(512)} fusion(s32[4]{0:T(128)S(1)} %copy-done.2, s32[1]{0:T(128)} %constant.60.clone.1, s32[1]{0:T(128)} %get-tuple-element.31, s32[1]{0:T(128)} %get-tuple-element.30), kind=kLoop, calls=%fused_computation.36 | loop fusion | flops 27 | bytes 29 | tf_op jit(solution)/shard_map/reduce.1
  69.1 0.1 reduce_sum.9
  69.2 14.3 %psum.15 = f32[64,128]{1,0:T(8,128)S(1)} all-reduce(f32[64,128]{1,0:T(8,128)S(1)} %reduce_sum.9), channel_id=1, replica_groups=mesh['zone'=4,'slab'=8] {'zone'}, use_global_device_ids=true, to_apply=%region_4.5 | all-reduce | flops 8192 | bytes 65536 | tf_op jit(solution)/shard_map/psum | solution.py:85
  83.5 0.0 collective-permute-done
  83.5 0.0 collective-permute-done.1
  83.5 0.0 copy-done.1
  83.5 21.2 %fusion.6 = f32[1,4,256,2048]{3,2,1,0:T(8,128)} fusion(f32[1,4,256,2048]{3,2,1,0:T(8,128)} %param.8, f32[1,4,1,2048]{3,2,1,0:T(1,128)S(1)} %collective-permute-done.1, f32[1,4,1,2048]{3,2,1,0:T(1,128)S(1)} %collective-permute-done, f32[1,4,256,1]{3,2,1,0:T(8,128)S(1)} %get-tuple-element.23, f32[1,4,256,2047]{3,2,1,0:T(8,128)} %get-tuple-element.25, ...), kind=kLoop, calls=%fused_computation.7 | loop fusion | flops 48234496 | bytes 42008592 | tf_op jit(solution)/shard_map/sub | solution.py:42
  104.7 0.0 reduce-scatter.2.cloned.1.call-done
  104.7 0.8 select_subtract_fusion
  105.5 0.1 copy.63
  105.6 0.1 copy.64
  105.7 0.1 reshape.156
  105.8 2.2 %broadcast_select_fusion = f32[1,4,1,2048]{3,2,1,0:T(1,128)S(1)} fusion(pred[]{:T(512)} %and_reduce_fusion, f32[1,4,1,2048]{3,2,1,0:T(1,128)S(1)} %reshape.156, f32[1,4,256,2048]{3,2,1,0:T(8,128)} %fusion.6, s32[]{:T(128)} %bitcast.4), kind=kLoop, calls=%fused_computation.31 | loop fusion | flops 16384 | bytes 98309 | tf_op jit(solution)/shard_map/select.1
  108.0 2.4 %scatter-add.4 = f32[1,4,256,2048]{3,2,1,0:T(8,128)} dynamic-update-slice(f32[1,4,256,2048]{3,2,1,0:T(8,128)} %fusion.6, f32[1,4,1,2048]{3,2,1,0:T(1,128)S(1)} %broadcast_select_fusion, s32[]{:T(128)} %constant.58.clone.1, s32[]{:T(128)} %constant.58.clone.1, s32[]{:T(128)} %bitcast.4, s32[]{:T(128)} %constant.58.clone.1) | dynamic-update-slice | bytes 65540 | tf_op jit(solution)/shard_map/scatter-add | solution.py:93
  (5 shorter events, 0.1 us)
Async XLA Ops:
  6.5 98.2 %reduce-scatter.2.cloned.1.call-start = ((), (), s32[]{:S(2)}) async-start(), calls=%async_computation.1 | async-start | bytes 294912 | tf_op jit(solution)/shard_map/reduce_scatter | solution.py:81
  43.0 40.5 %collective-permute-start = (f32[1,4,1,2048]{3,2,1,0:T(1,128)S(1)}, f32[1,4,1,2048]{3,2,1,0:T(1,128)S(1)}, u32[]{:S(2)}, u32[]{:S(2)}) collective-permute-start(f32[1,4,1,2048]{3,2,1,0:T(1,128)S(1)} %get-tuple-element.21), channel_id=1, source_target_pairs={{0,1},{1,2},{2,3},{3,4},{4,5},{5,6},{6,7},{8,9},{9,10},{10,11},{11... | collective-permute-start | bytes 98312 | tf_op jit(solution)/shard_map/ppermute | solution.py:15
  44.9 18.7 %copy-start = (f32[1,2,256,2048]{3,2,1,0:T(8,128)S(1)}, f32[1,2,256,2048]{3,2,1,0:T(8,128)}, u32[]{:S(2)}) copy-start(f32[1,2,256,2048]{3,2,1,0:T(8,128)} %param.9) | copy-start | bytes 12582916
  44.9 38.5 %collective-permute-start.1 = (f32[1,4,1,2048]{3,2,1,0:T(1,128)S(1)}, f32[1,4,1,2048]{3,2,1,0:T(1,128)S(1)}, u32[]{:S(2)}, u32[]{:S(2)}) collective-permute-start(f32[1,4,1,2048]{3,2,1,0:T(1,128)S(1)} %get-tuple-element.20), channel_id=1, source_target_pairs={{1,0},{2,1},{3,2},{4,3},{5,4},{6,5},{7,6},{9,8},{10,9},{11,10},{12... | collective-permute-start | bytes 98312 | tf_op jit(solution)/shard_map/ppermute | solution.py:18
  62.1 5.0 %copy-start.2 = (s32[4]{0:T(128)S(1)}, s32[4]{0:T(128)}, u32[]{:S(2)}) copy-start(s32[4]{0:T(128)} %constant.61.clone.1) | copy-start | bytes 52
  62.1 21.4 %copy-start.1 = (f32[4]{0:T(128)S(1)}, f32[4]{0:T(128)}, u32[]{:S(2)}) copy-start(f32[4]{0:T(128)} %param.10) | copy-start | bytes 52
Sparse Core Ops, SparseCore 0:
  43.1 26.0 reduce-scatter.1
where the time goes:
time: 118 us; the launch traced here: 117 us
  blocking collectives  45 us (38%)
  other arithmetic  29.1 us (25%)
  local copies, waits for them, and re-layouts  22.2 us (19%)
  between operations  13.5 us (11%)
  starting transfers between devices  5.83 us (5%)
  matrix products  1.48 us (1%)
    sub x1, other arithmetic, advance(): return center + diffusivity[None, :, None, None] * laplace - transport  21.2 us
    psum x1, blocking collectives, from_root(): return lax.psum(block, axis)  16.3 us
    slice x2, local copies, waits for them, and re-layouts, advance(): left_cells = jnp.roll(center, 1, axis=3)  14.7 us
    all_gather x1, blocking collectives, shards(): zone_faces = lax.all_gather(own_face, 'slab', axis=0, tiled=True)  14.4 us
    psum x1, blocking collectives, shards(): pin_total = lax.psum(pin_part, 'zone')  14.3 us
    another operation x3, other arithmetic  4.18 us
    ppermute x1, starting transfers between devices, extended(): lax.ppermute(lax.slice_in_dim(block, 0, width, axis=dim), axis, backward)  3.91 us
    mul x1, other arithmetic, advance(): jnp.maximum(along_rows, 0.0) * (center - upper_row)  2.91 us
  transfers between devices with their start and end apart: 3, of which 0 were waited for; matrix products, arithmetic and copies ran while one was open for 35% of the time, Pallas kernels for 0%

commit v1 on v0

--- a/solution.py
+++ b/solution.py
@@ -82,7 +82,7 @@
         jnp.dot(picker.T, item_flux, precision=highest), "slab", scatter_dimension=0, tiled=True
     )
     pin_part = jnp.sum(item_flux.reshape(seg_count, fanout, payload), axis=1)
-    pin_total = lax.psum(pin_part, "zone")
+    pin_total = jnp.sum(lax.all_gather(pin_part, "zone"), axis=0)
     is_pin = zone_index == zone_count - 1
     coupling = COUPLE * inflow - jnp.where(is_pin, COUPLE * pin_total, 0.0)
     coupling = (

time: 118 us -> 111 us (0.941)
  blocking collectives: 45 us -> 38.4 us
    psum x1 -> x0, blocking collectives: 14.3 us -> none  [shards(): pin_total = lax.psum(pin_part, 'zone')]
    all_gather x0 -> x1, blocking collectives: none -> 7.64 us  [shards(): pin_total = jnp.sum(lax.all_gather(pin_part, 'zone'), axis=0)]
  transfers between devices with their start and end apart: 3 -> 3, of which waited for: 0 -> 0; matrix products, arithmetic and copies ran while one was open for 35% -> 38% of each run, Pallas kernels for 0% -> 0%
where the time goes in v1:
time: 111 us
  blocking collectives  38.4 us (35%)
  other arithmetic  29.2 us (26%)
  local copies, waits for them, and re-layouts  22.2 us (20%)
  between operations  13.5 us (12%)
  starting transfers between devices  5.83 us (5%)
  matrix products  1.48 us (1%)
    sub x1, other arithmetic, advance(): return center + diffusivity[None, :, None, None] * laplace - transport  21.2 us
    psum x1, blocking collectives, from_root(): return lax.psum(block, axis)  16.3 us
    slice x2, local copies, waits for them, and re-layouts, advance(): left_cells = jnp.roll(center, 1, axis=3)  14.7 us
    all_gather x1, blocking collectives, shards(): zone_faces = lax.all_gather(own_face, 'slab', axis=0, tiled=True)  14.4 us
    all_gather x1, blocking collectives, shards(): pin_total = jnp.sum(lax.all_gather(pin_part, 'zone'), axis=0)  7.64 us
    another operation x3, other arithmetic  4.18 us
    ppermute x1, starting transfers between devices, extended(): lax.ppermute(lax.slice_in_dim(block, 0, width, axis=dim), axis, backward)  3.91 us
    mul x1, other arithmetic, advance(): jnp.maximum(along_rows, 0.0) * (center - upper_row)  2.91 us
  transfers between devices with their start and end apart: 3, of which 0 were waited for; matrix products, arithmetic and copies ran while one was open for 38% of the time, Pallas kernels for 0%

profile of v1, /device:TPU:8, one launch (start us, length us, event | category | flops | bytes accessed | tf_op | source)
XLA Modules:
  0.0 110.6 jit_solution(14113195860189836885)
XLA Ops:
  6.5 0.0 reduce-scatter.2.cloned.1.call-start
  6.5 1.2 %slice_reduce_fusion = (f32[4,2048]{1,0:T(4,128)S(1)}, f32[1,4,1,2048]{3,2,1,0:T(1,128)S(1)}, f32[1,4,1,2048]{3,2,1,0:T(1,128)S(1)}) fusion(f32[1,4,256,2048]{3,2,1,0:T(8,128)} %param.8), kind=kLoop, calls=%fused_computation.45 | loop fusion | bytes 163840 | tf_op jit(solution)/shard_map/slice | solution.py:16
  7.7 0.1 reshape_squeeze.3
  7.8 0.1 copy.83
  7.9 0.1 copy.84
  7.9 14.4 %all_gather.9 = f32[512,128]{1,0:T(8,128)S(1)} all-gather(f32[64,128]{1,0:T(8,128)S(1)} %copy.84), channel_id=1, replica_groups=mesh['zone'=4,'slab'=8] {'slab'}, dimensions={0}, use_global_device_ids=true | all-gather | bytes 294912 | tf_op jit(solution)/shard_map/all_gather | solution.py:74
  22.4 16.3 %psum.7 = f32[64,128]{1,0:T(8,128)S(1)} all-reduce(f32[64,128]{1,0:T(8,128)S(1)} %broadcast_select_fusion.1), channel_id=1, replica_groups=mesh['zone'=4,'slab'=8] {'zone'}, use_global_device_ids=true, to_apply=%region_1.2 | all-reduce | flops 8192 | bytes 65536 | tf_op jit(solution)/shard_map/psum | solution.py:25
  38.7 0.8 copy.80
  39.5 0.1 reshape.148
  39.6 0.8 copy.82
  40.4 0.1 reshape.150
  40.5 0.8 copy.81
  41.3 0.1 reshape.149
  41.5 0.3 fusion.14
  41.8 1.2 %fusion.16 = f32[512,128]{1,0:T(8,128)} fusion(f32[128,128]{1,0:T(8,128)S(1)} %fusion.14, s32[128]{0:T(128)S(1)} %fusion.24, pred[128]{0:T(512)(128)(4,1)S(1)} %get-tuple-element.18), kind=kOutput, calls=%fused_computation.26 | convolution fusion | flops 100794368 | bytes 328320 | tf_op jit(solution)/shard_map/dot_general | solution.py:82
  43.0 0.0 reduce-scatter.2.cloned.1.call-update
  43.0 1.9 %collective-permute-start = (f32[1,4,1,2048]{3,2,1,0:T(1,128)S(1)}, f32[1,4,1,2048]{3,2,1,0:T(1,128)S(1)}, u32[]{:S(2)}, u32[]{:S(2)}) collective-permute-start(f32[1,4,1,2048]{3,2,1,0:T(1,128)S(1)} %get-tuple-element.21), channel_id=1, source_target_pairs={{0,1},{1,2},{2,3},{3,4},{4,5},{5,6},{6,7},{8,9},{9,10},{10,11},{11... | collective-permute-start | bytes 98312 | tf_op jit(solution)/shard_map/ppermute | solution.py:15
  44.9 0.0 copy-start
  44.9 3.9 %collective-permute-start.1 = (f32[1,4,1,2048]{3,2,1,0:T(1,128)S(1)}, f32[1,4,1,2048]{3,2,1,0:T(1,128)S(1)}, u32[]{:S(2)}, u32[]{:S(2)}) collective-permute-start(f32[1,4,1,2048]{3,2,1,0:T(1,128)S(1)} %get-tuple-element.20), channel_id=1, source_target_pairs={{1,0},{2,1},{3,2},{4,3},{5,4},{6,5},{7,6},{9,8},{10,9},{11,10},{12... | collective-permute-start | bytes 98312 | tf_op jit(solution)/shard_map/ppermute | solution.py:18
  48.9 13.3 %fusion.28 = (f32[1,4,256,2047]{3,2,1,0:T(8,128)}, f32[1,4,256,2047]{3,2,1,0:T(8,128)}) fusion(f32[1,4,256,2048]{3,2,1,0:T(8,128)} %param.8), kind=kLoop, calls=%fused_computation.47 | loop fusion | bytes 33538048 | tf_op jit(solution)/shard_map/jit(_roll_static)/slice | solution.py:29
  62.1 0.0 copy-start.2
  62.1 0.0 copy-start.1
  62.1 1.4 %fusion.27 = (f32[1,4,256,1]{3,2,1,0:T(8,128)S(1)}, f32[1,4,256,1]{3,2,1,0:T(8,128)S(1)}) fusion(f32[1,4,256,2048]{3,2,1,0:T(8,128)} %param.8), kind=kLoop, calls=%fused_computation.46 | loop fusion | bytes 16384 | tf_op jit(solution)/shard_map/jit(_roll_static)/slice | solution.py:29
  63.6 0.0 copy-done
  63.6 2.9 %maximum_bitcast_fusion.1 = (f32[256,2048]{1,0:T(8,128)S(1)}, f32[256,2048]{1,0:T(8,128)}, f32[256,2048]{1,0:T(8,128)}, f32[256,2048]{1,0:T(8,128)}) fusion(f32[1,2,256,2048]{3,2,1,0:T(8,128)S(1)} %copy-done), kind=kLoop, calls=%fused_computation.21 | loop fusion | flops 2097152 | bytes 12582912 | tf_op jit(solution)/shard_map/mul | solution.py:33
  66.5 0.6 fusion.29
  67.1 0.0 copy-done.2
  67.1 2.0 %and_reduce_fusion = pred[]{:T(512)} fusion(s32[4]{0:T(128)S(1)} %copy-done.2, s32[1]{0:T(128)} %constant.60.clone.1, s32[1]{0:T(128)} %get-tuple-element.31, s32[1]{0:T(128)} %get-tuple-element.30), kind=kLoop, calls=%fused_computation.36 | loop fusion | flops 27 | bytes 29 | tf_op jit(solution)/shard_map/reduce.1
  69.1 0.1 reduce_sum.18
  69.2 7.6 %all-gather = f32[256,128]{1,0:T(8,128)S(1)} all-gather(f32[64,128]{1,0:T(8,128)S(1)} %reduce_sum.18), channel_id=2, replica_groups=mesh['zone'=4,'slab'=8] {'zone'}, dimensions={0}, use_global_device_ids=true | all-gather | bytes 163840 | tf_op jit(solution)/shard_map/all_gather | solution.py:85
  76.8 0.0 collective-permute-done
  76.8 0.0 collective-permute-done.1
  76.9 0.0 copy-done.1
  76.9 21.2 %fusion.6 = f32[1,4,256,2048]{3,2,1,0:T(8,128)} fusion(f32[1,4,256,2048]{3,2,1,0:T(8,128)} %param.8, f32[1,4,1,2048]{3,2,1,0:T(1,128)S(1)} %collective-permute-done.1, f32[1,4,1,2048]{3,2,1,0:T(1,128)S(1)} %collective-permute-done, f32[1,4,256,1]{3,2,1,0:T(8,128)S(1)} %get-tuple-element.23, f32[1,4,256,2047]{3,2,1,0:T(8,128)} %get-tuple-element.25, ...), kind=kLoop, calls=%fused_computation.7 | loop fusion | flops 48234496 | bytes 42008592 | tf_op jit(solution)/shard_map/sub | solution.py:42
  98.1 0.0 reduce-scatter.2.cloned.1.call-done
  98.1 0.8 select_subtract_fusion
  98.8 0.1 copy.86
  98.9 0.1 copy.87
  99.0 0.1 reshape.157
  99.2 2.2 %broadcast_select_fusion = f32[1,4,1,2048]{3,2,1,0:T(1,128)S(1)} fusion(pred[]{:T(512)} %and_reduce_fusion, f32[1,4,1,2048]{3,2,1,0:T(1,128)S(1)} %reshape.157, f32[1,4,256,2048]{3,2,1,0:T(8,128)} %fusion.6, s32[]{:T(128)} %bitcast.4), kind=kLoop, calls=%fused_computation.31 | loop fusion | flops 16384 | bytes 98309 | tf_op jit(solution)/shard_map/select.1
  101.3 2.4 %scatter-add.4 = f32[1,4,256,2048]{3,2,1,0:T(8,128)} dynamic-update-slice(f32[1,4,256,2048]{3,2,1,0:T(8,128)} %fusion.6, f32[1,4,1,2048]{3,2,1,0:T(1,128)S(1)} %broadcast_select_fusion, s32[]{:T(128)} %constant.58.clone.1, s32[]{:T(128)} %constant.58.clone.1, s32[]{:T(128)} %bitcast.4, s32[]{:T(128)} %constant.58.clone.1) | dynamic-update-slice | bytes 65540 | tf_op jit(solution)/shard_map/scatter-add | solution.py:93
  (6 shorter events, 0.1 us)
Async XLA Ops:
  6.5 91.5 %reduce-scatter.2.cloned.1.call-start = ((), (), s32[]{:S(2)}) async-start(), calls=%async_computation.1 | async-start | bytes 294912 | tf_op jit(solution)/shard_map/reduce_scatter | solution.py:81
  43.0 33.8 %collective-permute-start = (f32[1,4,1,2048]{3,2,1,0:T(1,128)S(1)}, f32[1,4,1,2048]{3,2,1,0:T(1,128)S(1)}, u32[]{:S(2)}, u32[]{:S(2)}) collective-permute-start(f32[1,4,1,2048]{3,2,1,0:T(1,128)S(1)} %get-tuple-element.21), channel_id=1, source_target_pairs={{0,1},{1,2},{2,3},{3,4},{4,5},{5,6},{6,7},{8,9},{9,10},{10,11},{11... | collective-permute-start | bytes 98312 | tf_op jit(solution)/shard_map/ppermute | solution.py:15
  44.9 18.7 %copy-start = (f32[1,2,256,2048]{3,2,1,0:T(8,128)S(1)}, f32[1,2,256,2048]{3,2,1,0:T(8,128)}, u32[]{:S(2)}) copy-start(f32[1,2,256,2048]{3,2,1,0:T(8,128)} %param.9) | copy-start | bytes 12582916
  44.9 31.9 %collective-permute-start.1 = (f32[1,4,1,2048]{3,2,1,0:T(1,128)S(1)}, f32[1,4,1,2048]{3,2,1,0:T(1,128)S(1)}, u32[]{:S(2)}, u32[]{:S(2)}) collective-permute-start(f32[1,4,1,2048]{3,2,1,0:T(1,128)S(1)} %get-tuple-element.20), channel_id=1, source_target_pairs={{1,0},{2,1},{3,2},{4,3},{5,4},{6,5},{7,6},{9,8},{10,9},{11,10},{12... | collective-permute-start | bytes 98312 | tf_op jit(solution)/shard_map/ppermute | solution.py:18
  62.1 5.0 %copy-start.2 = (s32[4]{0:T(128)S(1)}, s32[4]{0:T(128)}, u32[]{:S(2)}) copy-start(s32[4]{0:T(128)} %constant.61.clone.1) | copy-start | bytes 52
  62.1 14.7 %copy-start.1 = (f32[4]{0:T(128)S(1)}, f32[4]{0:T(128)}, u32[]{:S(2)}) copy-start(f32[4]{0:T(128)} %param.10) | copy-start | bytes 52
Sparse Core Ops, SparseCore 0:
  43.1 26.0 reduce-scatter.1
